TPU v7x, 128 devices: a whole 4x4x4 slice. The times are simulated.
128 devices in a mesh: leaf: 8 (over y, core), front: 16 (over z, x).
Axes of the slice: x: 4, y: 4, z: 4, core: 2. Of those that a mesh axis runs over, the one named last changes fastest.
Arguments:
- front_entries: float32 [16, 8, 128, 8, 16, 128], P(None, 'leaf', None, None, 'front'), as said below
- child_panels: bfloat16 [8, 2048, 512], P('leaf', 'front'), may hold values from -0.053955078 to 0.053955078
- child_blocks: bfloat16 [8, 2048, 2048], P('leaf', None, 'front'), as said below
- child_map: int32 [8, 16], replicated, may hold values from 0 to 127, as said below
Outputs:
- factored: float32 [16, 8, 128, 8, 16, 128], P(None, 'leaf', None, None, 'front')
Inputs may be any that keep to these rules, and one draw needn't show every extreme that they name: The blocks of one subtree go to distinct parent blocks, and child_map[c, j] modulo 16 equals j. front_entries is symmetric and positive definite, with its diagonal in 6 to 9. `child_blocks`: each subtree's block is symmetric with diagonal in 6 to 9 and small independent entries elsewhere.
All inputs are finite; a program needn't handle non-finite values.
Results may differ from a plain program's by a relative error of at most 0.0012.
Values may be sent and summed in bfloat16 or wider, within the bound.
No kernel may reach another device: no remote copies, remote signals or barrier semaphores. Data moves between devices by JAX's collectives and lax.ppermute only.
A program may use at most 128 MiB of HBM per device.

v0:
```python
import jax
import jax.numpy as jnp
from jax import lax
from jax.sharding import PartitionSpec as P

KS = 8


def broadcast(x, axis, root):
    mine = lax.axis_index(axis) == root
    return lax.psum(jnp.where(mine, x, jnp.zeros_like(x)), axis)


def for_sending(x):
    return jax.tree.map(lambda a: a.astype(jnp.bfloat16) if a.dtype == jnp.float32 else a, x)


def on_device(front_entries, child_panels, child_blocks, child_map):
    leaf_count = lax.axis_size("leaf")
    front_count = lax.axis_size("front")
    leaf_id = lax.axis_index("leaf")
    front_id = lax.axis_index("front")
    row_blocks = front_entries.shape[0]
    block_size = front_entries.shape[2]
    col_blocks = front_entries.shape[3]
    spread = front_count // leaf_count
    own_rows = child_panels[0]
    own_block = child_blocks[0]
    given = own_block.astype(jnp.float32)
    product = lax.dot_general(
        lax.all_gather(child_panels[0], "front", axis=0, tiled=True),
        own_rows,
        (((1,), (1,)), ((), ())),
        preferred_element_type=jnp.float32,
    )
    update = (given - product).astype(jnp.bfloat16)
    row_targets = lax.dynamic_index_in_dim(
        child_map.reshape(leaf_count, spread, leaf_count), leaf_id, 2, keepdims=False
    )
    col_targets = lax.dynamic_index_in_dim(child_map, front_id, 1, keepdims=False)
    row_onehot = (
        row_targets[:, :, None] // leaf_count == jnp.arange(row_blocks)[None, None, :]
    ).astype(jnp.float32)
    col_onehot = (col_targets[:, None] // front_count == jnp.arange(col_blocks)[None, :]).astype(
        jnp.float32
    )
    every = lax.all_gather(update[None], "leaf", axis=0, tiled=True)
    received = lax.dynamic_index_in_dim(
        every.reshape(leaf_count, spread, leaf_count, block_size, block_size),
        leaf_id,
        2,
        keepdims=False,
    )
    added = jnp.einsum(
        "cqr,cqxy,cs->rxsy",
        row_onehot,
        received.astype(jnp.float32),
        col_onehot,
        precision=lax.Precision.HIGHEST,
    )
    assembled = front_entries.reshape(
        row_blocks * block_size, col_blocks * block_size
    ) + added.reshape(row_blocks * block_size, col_blocks * block_size)
    global_rows = jnp.arange(row_blocks) * leaf_count + leaf_id
    global_cols = jnp.arange(col_blocks) * front_count + front_id
    for pivot_index in range(KS):
        col_local = pivot_index // front_count
        col_owner = pivot_index % front_count
        row_local = pivot_index // leaf_count
        row_owner = pivot_index % leaf_count
        column = assembled[:, col_local * block_size : (col_local + 1) * block_size]
        panel = broadcast(column.astype(jnp.bfloat16), "front", col_owner).astype(column.dtype)
        pivot = broadcast(
            panel[row_local * block_size : (row_local + 1) * block_size].astype(jnp.bfloat16),
            "leaf",
            row_owner,
        ).astype(jnp.float32)
        factor = jnp.linalg.cholesky(pivot)
        solved = lax.linalg.triangular_solve(
            factor, panel, left_side=False, lower=True, transpose_a=True
        )
        keeping = (global_rows >= pivot_index).astype(jnp.float32)
        solved = (
            solved.reshape(row_blocks, block_size, block_size) * keeping[:, None, None]
        ).reshape(row_blocks * block_size, block_size)
        chosen = lax.dynamic_index_in_dim(
            solved.reshape(col_blocks, spread, block_size, block_size),
            front_id // leaf_count,
            1,
            keepdims=False,
        )
        matching = broadcast(for_sending(chosen), "leaf", front_id % leaf_count).astype(
            chosen.dtype
        )
        assembled = assembled - lax.dot_general(
            solved,
            matching.reshape(col_blocks * block_size, block_size),
            (((1,), (1,)), ((), ())),
            precision=lax.Precision.HIGHEST,
            preferred_element_type=jnp.float32,
        )
        current = assembled[:, col_local * block_size : (col_local + 1) * block_size]
        assembled = assembled.at[:, col_local * block_size : (col_local + 1) * block_size].set(
            jnp.where(front_id == col_owner, solved, current)
        )
    shaped = assembled.reshape(row_blocks, block_size, col_blocks, block_size)
    keep_rows = global_rows[:, None] >= KS
    keep_cols = global_cols[None, :] < KS
    keeping = jnp.logical_or(keep_rows, keep_cols)
    result = jnp.where(keeping[:, None, :, None], shaped, 0.0)
    return result.reshape(row_blocks, 1, block_size, col_blocks, 1, block_size)


def solution(mesh):
    placed = (
        P(None, "leaf", None, None, "front", None),
        P("leaf", "front", None),
        P("leaf", None, "front"),
        P(),
    )
    return jax.shard_map(
        on_device,
        mesh=mesh,
        in_specs=placed,
        out_specs=P(None, "leaf", None, None, "front", None),
        check_vma=False,
    )
```

profile of v0, /device:TPU:0, one launch (start us, length us, event | category | flops | bytes accessed | tf_op | source)
XLA Modules:
  0.0 1841.0 jit_solution(18026250259954352641)
XLA Ops:
  7.3 49.7 %all-gather.5.cloned.1.call-done = bf16[1,2048,512]{2,1,0:T(8,128)(2,1)} async-done(((bf16[1,128,512]{2,1,0:T(8,128)(2,1)}), bf16[1,2048,512]{2,1,0:T(8,128)(2,1)}) %all-gather.5.cloned.1.call-update) | async-done | bytes 2097168 | tf_op jit(solution)/shard_map/all_gather | solution.py:31
  79.8 12.0 all-gather.7.cloned.1.call-done
  103.6 25.1 %copy.29 = f32[16,128,8,128]{1,0,3,2:T(8,128)} copy(f32[16,128,8,128]{3,2,0,1:T(8,128)} %fusion.2) | data formatting | bytes 16777216 | tf_op jit(solution)/shard_map/cqr,cqxy,cs->rxsy/transpose | solution.py:54
  128.7 13.9 bitcast_add_fusion
  144.9 85.7 %all-reduce.17.cloned.1.call-done = bf16[2048,128]{0,1:T(8,128)(2,1)} async-done(((bf16[2048,128]{0,1:T(8,128)(2,1)}), bf16[2048,128]{0,1:T(8,128)(2,1)}) %all-reduce.17.cloned.1.call-update) | async-done | bytes 524304 | tf_op jit(solution)/shard_map/psum | solution.py:11
  231.4 23.6 %psum.169 = bf16[128,128]{0,1:T(8,128)(2,1)S(1)} all-reduce(bf16[128,128]{0,1:T(8,128)(2,1)S(1)} %slice_select_fusion.7), channel_id=1, replica_groups=mesh['leaf'=8,'front'=16] {'leaf'}, use_global_device_ids=true, to_apply=%region_1.2 | all-reduce | flops 16384 | bytes 65536 | tf_op jit(solution)/shard_map/psum | solution.py:11
  255.1 11.7 cholesky.134
  283.7 56.6 %all-reduce.19.cloned.1.call-done = bf16[1024,128]{1,0:T(8,128)(2,1)} async-done(((bf16[1024,128]{1,0:T(8,128)(2,1)}), bf16[1024,128]{1,0:T(8,128)(2,1)}) %all-reduce.19.cloned.1.call-update) | async-done | bytes 262160 | tf_op jit(solution)/shard_map/psum | solution.py:11
  351.9 84.8 %all-reduce.21.cloned.1.call-done = bf16[2048,128]{0,1:T(8,128)(2,1)} async-done(((bf16[2048,128]{0,1:T(8,128)(2,1)}), bf16[2048,128]{0,1:T(8,128)(2,1)}) %all-reduce.21.cloned.1.call-update) | async-done | bytes 524304 | tf_op jit(solution)/shard_map/psum | solution.py:11
  437.5 24.1 %psum.172 = bf16[128,128]{0,1:T(8,128)(2,1)S(1)} all-reduce(bf16[128,128]{0,1:T(8,128)(2,1)S(1)} %slice_select_fusion.6), channel_id=1, replica_groups=mesh['leaf'=8,'front'=16] {'leaf'}, use_global_device_ids=true, to_apply=%region_7.10 | all-reduce | flops 16384 | bytes 65536 | tf_op jit(solution)/shard_map/psum | solution.py:11
  461.8 11.7 cholesky.145
  494.2 54.3 %all-reduce.23.cloned.1.call-done = bf16[1024,128]{1,0:T(8,128)(2,1)} async-done(((bf16[1024,128]{1,0:T(8,128)(2,1)}), bf16[1024,128]{1,0:T(8,128)(2,1)}) %all-reduce.23.cloned.1.call-update) | async-done | bytes 262160 | tf_op jit(solution)/shard_map/psum | solution.py:11
  560.1 84.9 %all-reduce.25.cloned.1.call-done = bf16[2048,128]{0,1:T(8,128)(2,1)} async-done(((bf16[2048,128]{0,1:T(8,128)(2,1)}), bf16[2048,128]{0,1:T(8,128)(2,1)}) %all-reduce.25.cloned.1.call-update) | async-done | bytes 524304 | tf_op jit(solution)/shard_map/psum | solution.py:11
  645.8 23.9 %psum.175 = bf16[128,128]{0,1:T(8,128)(2,1)S(1)} all-reduce(bf16[128,128]{0,1:T(8,128)(2,1)S(1)} %slice_select_fusion.5), channel_id=1, replica_groups=mesh['leaf'=8,'front'=16] {'leaf'}, use_global_device_ids=true, to_apply=%region_10.13 | all-reduce | flops 16384 | bytes 65536 | tf_op jit(solution)/shard_map/psum | solution.py:11
  669.8 11.7 cholesky.156
  702.2 54.4 %all-reduce.27.cloned.1.call-done = bf16[1024,128]{1,0:T(8,128)(2,1)} async-done(((bf16[1024,128]{1,0:T(8,128)(2,1)}), bf16[1024,128]{1,0:T(8,128)(2,1)}) %all-reduce.27.cloned.1.call-update) | async-done | bytes 262160 | tf_op jit(solution)/shard_map/psum | solution.py:11
  768.2 84.8 %all-reduce.29.cloned.1.call-done = bf16[2048,128]{0,1:T(8,128)(2,1)} async-done(((bf16[2048,128]{0,1:T(8,128)(2,1)}), bf16[2048,128]{0,1:T(8,128)(2,1)}) %all-reduce.29.cloned.1.call-update) | async-done | bytes 524304 | tf_op jit(solution)/shard_map/psum | solution.py:11
  853.8 24.0 %psum.178 = bf16[128,128]{0,1:T(8,128)(2,1)S(1)} all-reduce(bf16[128,128]{0,1:T(8,128)(2,1)S(1)} %slice_select_fusion.4), channel_id=1, replica_groups=mesh['leaf'=8,'front'=16] {'leaf'}, use_global_device_ids=true, to_apply=%region_13.16 | all-reduce | flops 16384 | bytes 65536 | tf_op jit(solution)/shard_map/psum | solution.py:11
  910.3 54.3 %all-reduce.31.cloned.1.call-done = bf16[1024,128]{1,0:T(8,128)(2,1)} async-done(((bf16[1024,128]{1,0:T(8,128)(2,1)}), bf16[1024,128]{1,0:T(8,128)(2,1)}) %all-reduce.31.cloned.1.call-update) | async-done | bytes 262160 | tf_op jit(solution)/shard_map/psum | solution.py:11
  976.3 84.9 %all-reduce.33.cloned.1.call-done = bf16[2048,128]{0,1:T(8,128)(2,1)} async-done(((bf16[2048,128]{0,1:T(8,128)(2,1)}), bf16[2048,128]{0,1:T(8,128)(2,1)}) %all-reduce.33.cloned.1.call-update) | async-done | bytes 524304 | tf_op jit(solution)/shard_map/psum | solution.py:11
  1061.9 24.1 %psum.181 = bf16[128,128]{0,1:T(8,128)(2,1)S(1)} all-reduce(bf16[128,128]{0,1:T(8,128)(2,1)S(1)} %slice_select_fusion.3), channel_id=1, replica_groups=mesh['leaf'=8,'front'=16] {'leaf'}, use_global_device_ids=true, to_apply=%region_16.19 | all-reduce | flops 16384 | bytes 65536 | tf_op jit(solution)/shard_map/psum | solution.py:11
  1118.6 54.4 %all-reduce.35.cloned.1.call-done = bf16[1024,128]{1,0:T(8,128)(2,1)} async-done(((bf16[1024,128]{1,0:T(8,128)(2,1)}), bf16[1024,128]{1,0:T(8,128)(2,1)}) %all-reduce.35.cloned.1.call-update) | async-done | bytes 262160 | tf_op jit(solution)/shard_map/psum | solution.py:11
  1184.6 84.8 %all-reduce.37.cloned.1.call-done = bf16[2048,128]{0,1:T(8,128)(2,1)} async-done(((bf16[2048,128]{0,1:T(8,128)(2,1)}), bf16[2048,128]{0,1:T(8,128)(2,1)}) %all-reduce.37.cloned.1.call-update) | async-done | bytes 524304 | tf_op jit(solution)/shard_map/psum | solution.py:11
  1270.2 23.9 %psum.184 = bf16[128,128]{0,1:T(8,128)(2,1)S(1)} all-reduce(bf16[128,128]{0,1:T(8,128)(2,1)S(1)} %slice_select_fusion.2), channel_id=1, replica_groups=mesh['leaf'=8,'front'=16] {'leaf'}, use_global_device_ids=true, to_apply=%region_19.22 | all-reduce | flops 16384 | bytes 65536 | tf_op jit(solution)/shard_map/psum | solution.py:11
  1326.6 54.4 %all-reduce.39.cloned.1.call-done = bf16[1024,128]{1,0:T(8,128)(2,1)} async-done(((bf16[1024,128]{1,0:T(8,128)(2,1)}), bf16[1024,128]{1,0:T(8,128)(2,1)}) %all-reduce.39.cloned.1.call-update) | async-done | bytes 262160 | tf_op jit(solution)/shard_map/psum | solution.py:11
  1392.7 84.8 %all-reduce.41.cloned.1.call-done = bf16[2048,128]{0,1:T(8,128)(2,1)} async-done(((bf16[2048,128]{0,1:T(8,128)(2,1)}), bf16[2048,128]{0,1:T(8,128)(2,1)}) %all-reduce.41.cloned.1.call-update) | async-done | bytes 524304 | tf_op jit(solution)/shard_map/psum | solution.py:11
  1478.3 24.0 %psum.187 = bf16[128,128]{0,1:T(8,128)(2,1)S(1)} all-reduce(bf16[128,128]{0,1:T(8,128)(2,1)S(1)} %slice_select_fusion.1), channel_id=1, replica_groups=mesh['leaf'=8,'front'=16] {'leaf'}, use_global_device_ids=true, to_apply=%region_22.25 | all-reduce | flops 16384 | bytes 65536 | tf_op jit(solution)/shard_map/psum | solution.py:11
  1534.7 54.3 %all-reduce.43.cloned.1.call-done = bf16[1024,128]{1,0:T(8,128)(2,1)} async-done(((bf16[1024,128]{1,0:T(8,128)(2,1)}), bf16[1024,128]{1,0:T(8,128)(2,1)}) %all-reduce.43.cloned.1.call-update) | async-done | bytes 262160 | tf_op jit(solution)/shard_map/psum | solution.py:11
  1600.7 84.8 %all-reduce.45.cloned.1.call-done = bf16[2048,128]{0,1:T(8,128)(2,1)} async-done(((bf16[2048,128]{0,1:T(8,128)(2,1)}), bf16[2048,128]{0,1:T(8,128)(2,1)}) %all-reduce.45.cloned.1.call-update) | async-done | bytes 524304 | tf_op jit(solution)/shard_map/psum | solution.py:11
  1686.3 24.1 %psum.190 = bf16[128,128]{0,1:T(8,128)(2,1)S(1)} all-reduce(bf16[128,128]{0,1:T(8,128)(2,1)S(1)} %slice_select_fusion), channel_id=1, replica_groups=mesh['leaf'=8,'front'=16] {'leaf'}, use_global_device_ids=true, to_apply=%region_25.28 | all-reduce | flops 16384 | bytes 65536 | tf_op jit(solution)/shard_map/psum | solution.py:11
  1742.9 54.5 %all-reduce.47.cloned.1.call-done = bf16[1024,128]{1,0:T(8,128)(2,1)} async-done(((bf16[1024,128]{1,0:T(8,128)(2,1)}), bf16[1024,128]{1,0:T(8,128)(2,1)}) %all-reduce.47.cloned.1.call-update) | async-done | bytes 262160 | tf_op jit(solution)/shard_map/psum | solution.py:11
  1810.3 13.3 copy.54
  (226 shorter events, 368.6 us)
Async XLA Ops:
  6.5 50.5 %all-gather.5.cloned.1.call-start = ((), (), s32[]{:S(2)}) async-start(), calls=%async_computation.16 | async-start | bytes 2228224 | tf_op jit(solution)/shard_map/all_gather | solution.py:31
  7.3 84.5 %all-gather.7.cloned.1.call-start = ((), (), s32[]{:S(2)}) async-start(), calls=%async_computation.17 | async-start | bytes 4718592 | tf_op jit(solution)/shard_map/all_gather | solution.py:47
  60.3 170.3 %all-reduce.17.cloned.1.call-start = ((), (), s32[]{:S(2)}) async-start(), calls=%async_computation | async-start | bytes 1048576 | tf_op jit(solution)/shard_map/psum | solution.py:11
  70.3 9.2 copy-start.7
  144.7 195.6 %all-reduce.19.cloned.1.call-start = ((), (), s32[]{:S(2)}) async-start(), calls=%async_computation.1 | async-start | bytes 524288 | tf_op jit(solution)/shard_map/psum | solution.py:11
  282.8 153.9 %all-reduce.21.cloned.1.call-start = ((), (), s32[]{:S(2)}) async-start(), calls=%async_computation.2 | async-start | bytes 1048576 | tf_op jit(solution)/shard_map/psum | solution.py:11
  346.6 3.4 copy-start.2
  351.8 196.7 %all-reduce.23.cloned.1.call-start = ((), (), s32[]{:S(2)}) async-start(), calls=%async_computation.3 | async-start | bytes 524288 | tf_op jit(solution)/shard_map/psum | solution.py:11
  491.1 153.9 %all-reduce.25.cloned.1.call-start = ((), (), s32[]{:S(2)}) async-start(), calls=%async_computation.4 | async-start | bytes 1048576 | tf_op jit(solution)/shard_map/psum | solution.py:11
  554.9 3.4 copy-start.3
  560.0 196.6 %all-reduce.27.cloned.1.call-start = ((), (), s32[]{:S(2)}) async-start(), calls=%async_computation.5 | async-start | bytes 524288 | tf_op jit(solution)/shard_map/psum | solution.py:11
  699.1 154.0 %all-reduce.29.cloned.1.call-start = ((), (), s32[]{:S(2)}) async-start(), calls=%async_computation.6 | async-start | bytes 1048576 | tf_op jit(solution)/shard_map/psum | solution.py:11
  762.9 3.4 copy-start.4
  768.1 196.6 %all-reduce.31.cloned.1.call-start = ((), (), s32[]{:S(2)}) async-start(), calls=%async_computation.7 | async-start | bytes 524288 | tf_op jit(solution)/shard_map/psum | solution.py:11
  907.2 153.9 %all-reduce.33.cloned.1.call-start = ((), (), s32[]{:S(2)}) async-start(), calls=%async_computation.8 | async-start | bytes 1048576 | tf_op jit(solution)/shard_map/psum | solution.py:11
  971.0 3.4 copy-start.5
  976.1 196.9 %all-reduce.35.cloned.1.call-start = ((), (), s32[]{:S(2)}) async-start(), calls=%async_computation.9 | async-start | bytes 524288 | tf_op jit(solution)/shard_map/psum | solution.py:11
  1115.5 154.0 %all-reduce.37.cloned.1.call-start = ((), (), s32[]{:S(2)}) async-start(), calls=%async_computation.10 | async-start | bytes 1048576 | tf_op jit(solution)/shard_map/psum | solution.py:11
  1179.3 3.4 copy-start.6
  1184.4 196.6 %all-reduce.39.cloned.1.call-start = ((), (), s32[]{:S(2)}) async-start(), calls=%async_computation.11 | async-start | bytes 524288 | tf_op jit(solution)/shard_map/psum | solution.py:11
  1323.5 153.9 %all-reduce.41.cloned.1.call-start = ((), (), s32[]{:S(2)}) async-start(), calls=%async_computation.12 | async-start | bytes 1048576 | tf_op jit(solution)/shard_map/psum | solution.py:11
  1387.4 3.4 copy-start
  1392.5 196.6 %all-reduce.43.cloned.1.call-start = ((), (), s32[]{:S(2)}) async-start(), calls=%async_computation.13 | async-start | bytes 524288 | tf_op jit(solution)/shard_map/psum | solution.py:11
  1531.7 153.9 %all-reduce.45.cloned.1.call-start = ((), (), s32[]{:S(2)}) async-start(), calls=%async_computation.14 | async-start | bytes 1048576 | tf_op jit(solution)/shard_map/psum | solution.py:11
  1595.4 3.4 copy-start.1
  1600.5 196.9 %all-reduce.47.cloned.1.call-start = ((), (), s32[]{:S(2)}) async-start(), calls=%async_computation.15 | async-start | bytes 524288 | tf_op jit(solution)/shard_map/psum | solution.py:11
Sparse Core Ops, SparseCore 0:
  9.5 47.4 all-gather.4
  60.4 31.3 all-gather.6
  144.8 85.7 all-reduce.16
  282.9 57.3 all-reduce.18
  351.9 84.8 all-reduce.20
  491.2 57.2 all-reduce.22
  560.1 84.8 all-reduce.24
  699.2 57.3 all-reduce.26
  768.2 84.8 all-reduce.28
  907.3 57.2 all-reduce.30
  976.2 84.8 all-reduce.32
  1115.6 57.3 all-reduce.34
  1184.6 84.8 all-reduce.36
  1323.7 57.3 all-reduce.38
  1392.6 84.8 all-reduce.40
  1531.8 57.2 all-reduce.42
  1600.6 84.8 all-reduce.44
  1740.0 57.3 all-reduce.46
where the time goes:
time: 1850 us; the launch traced here: 1840 us
  waiting for transfers between devices  1180 us (64%)
  other arithmetic  258 us (14%)
  blocking collectives  192 us (10%)
  local copies, waits for them, and re-layouts  114 us (6%)
  matrix products  81.6 us (4%)
    psum x16, waiting for transfers between devices, broadcast(): return lax.psum(jnp.where(mine, x, jnp.zeros_like(x)), axis)  1120 us
    psum x8, blocking collectives, broadcast(): return lax.psum(jnp.where(mine, x, jnp.zeros_like(x)), axis)  192 us
    another operation x24, other arithmetic, on_device(): factor = jnp.linalg.cholesky(pivot)  99.8 us
    another operation x16, other arithmetic, on_device(): lax.linalg.triangular_solve(factor, panel, left_side=False, lower=True, t...  84.1 us
    dot_general x8, matrix products, on_device(): lax.dot_general(solved, matching.reshape(col_blocks * block_size, block_s...  50.9 us
    all_gather x1, waiting for transfers between devices, on_device(): lax.all_gather(child_panels[0], 'front', axis=0, tiled=True)  49.7 us
    unnamed x26, local copies, waits for them, and re-layouts  47.1 us
  transfers between devices with their start and end apart: 18, of which 18 were waited for; matrix products, arithmetic and copies ran while one was open for 2% of the time, Pallas kernels for 0%

commit v1 on v0

--- a/solution.py
+++ b/solution.py
@@ -8,7 +8,7 @@
 
 def broadcast(x, axis, root):
     mine = lax.axis_index(axis) == root
-    return lax.psum(jnp.where(mine, x, jnp.zeros_like(x)), axis)
+    return jnp.sum(lax.all_gather(jnp.where(mine, x, jnp.zeros_like(x)), axis), axis=0)
 
 
 def for_sending(x):

time: 1850 us -> 1520 us (0.82)
  waiting for transfers between devices: 1180 us -> 802 us
  blocking collectives: 192 us -> 99.9 us
  other arithmetic: 258 us -> 328 us
  local copies, waits for them, and re-layouts: 114 us -> 184 us
    psum x16 -> x0, waiting for transfers between devices: 1120 us -> none  [broadcast(): return lax.psum(jnp.where(mine, x, jnp.zeros_like(x)), axis)]
    all_gather x0 -> x16, waiting for transfers between devices: none -> 739 us  [broadcast(): lax.all_gather(jnp.where(mine, x, jnp.zeros_like(x)), axis)]
    psum x8 -> x0, blocking collectives: 192 us -> none  [broadcast(): return lax.psum(jnp.where(mine, x, jnp.zeros_like(x)), axis)]
    all_gather x0 -> x8, blocking collectives: none -> 99.9 us  [broadcast(): lax.all_gather(jnp.where(mine, x, jnp.zeros_like(x)), axis)]
    unnamed x26 -> x34, local copies, waits for them, and re-layouts: 47.1 us -> 141 us
    reduce_sum x0 -> x24, other arithmetic: none -> 77.5 us  [broadcast(): jnp.sum(lax.all_gather(jnp.where(mine, x, jnp.zeros_like(x)), axis), axis=0)]
    transpose x1 -> x0, local copies, waits for them, and re-layouts: 25.1 us -> none  [on_device(): jnp.einsum('cqr,cqxy,cs->rxsy', row_onehot, received.astype(jnp.float32),...]
  transfers between devices with their start and end apart: 18 -> 18, of which waited for: 18 -> 18; matrix products, arithmetic and copies ran while one was open for 2% -> 3% of each run, Pallas kernels for 0% -> 0%
where the time goes in v1:
time: 1520 us; the launch traced here: 1510 us
  waiting for transfers between devices  802 us (53%)
  other arithmetic  328 us (22%)
  local copies, waits for them, and re-layouts  184 us (12%)
  blocking collectives  99.9 us (7%)
  matrix products  73.3 us (5%)
    all_gather x16, waiting for transfers between devices, broadcast(): lax.all_gather(jnp.where(mine, x, jnp.zeros_like(x)), axis)  739 us
    unnamed x34, local copies, waits for them, and re-layouts  141 us
    all_gather x8, blocking collectives, broadcast(): lax.all_gather(jnp.where(mine, x, jnp.zeros_like(x)), axis)  99.9 us
    another operation x24, other arithmetic, on_device(): factor = jnp.linalg.cholesky(pivot)  99.7 us
    another operation x16, other arithmetic, on_device(): lax.linalg.triangular_solve(factor, panel, left_side=False, lower=True, t...  84.1 us
    reduce_sum x24, other arithmetic, broadcast(): jnp.sum(lax.all_gather(jnp.where(mine, x, jnp.zeros_like(x)), axis), axis=0)  77.5 us
    dot_general x8, matrix products, on_device(): lax.dot_general(solved, matching.reshape(col_blocks * block_size, block_s...  50.9 us
    all_gather x1, waiting for transfers between devices, on_device(): lax.all_gather(child_panels[0], 'front', axis=0, tiled=True)  49.7 us
  transfers between devices with their start and end apart: 18, of which 18 were waited for; matrix products, arithmetic and copies ran while one was open for 3% of the time, Pallas kernels for 0%

profile of v1, /device:TPU:0, one launch (start us, length us, event | category | flops | bytes accessed | tf_op | source)
XLA Modules:
  0.0 1505.4 jit_solution(13356152838877306854)
XLA Ops:
  7.3 49.7 %all-gather.45.cloned.1.call-done = bf16[1,2048,512]{2,1,0:T(8,128)(2,1)} async-done(((bf16[1,128,512]{2,1,0:T(8,128)(2,1)}), bf16[1,2048,512]{2,1,0:T(8,128)(2,1)}) %all-gather.45.cloned.1.call-update) | async-done | bytes 2097168 | tf_op jit(solution)/shard_map/all_gather | solution.py:31
  79.1 12.7 all-gather.47.cloned.1.call-done
  103.6 14.1 copy.98
  117.7 13.9 bitcast_add_fusion
  133.9 70.9 %all-gather.49.cloned.1.call-done = bf16[32768,128]{0,1:T(8,128)(2,1)} async-done(((bf16[2048,128]{0,1:T(8,128)(2,1)}), bf16[32768,128]{0,1:T(8,128)(2,1)}) %all-gather.49.cloned.1.call-update) | async-done | bytes 8388624 | tf_op jit(solution)/shard_map/all_gather | solution.py:11
  204.8 12.9 copy.110
  264.0 23.3 %all-gather.51.cloned.1.call-done = bf16[64,1,128,128]{3,2,1,0:T(8,128)(2,1)} async-done(((bf16[8,1,128,128]{3,2,1,0:T(8,128)(2,1)}), bf16[64,1,128,128]{3,2,1,0:T(8,128)(2,1)}) %all-gather.51.cloned.1.call-update) | async-done | bytes 2097168 | tf_op jit(solution)/shard_map/all_gather | solution.py:11
  301.0 71.1 %all-gather.53.cloned.1.call-done = bf16[32768,128]{0,1:T(8,128)(2,1)} async-done(((bf16[2048,128]{0,1:T(8,128)(2,1)}), bf16[32768,128]{0,1:T(8,128)(2,1)}) %all-gather.53.cloned.1.call-update) | async-done | bytes 8388624 | tf_op jit(solution)/shard_map/all_gather | solution.py:11
  372.2 12.9 copy.112
  392.6 12.6 all-gather.6
  433.9 21.0 %all-gather.55.cloned.1.call-done = bf16[64,1,128,128]{3,2,1,0:T(8,128)(2,1)} async-done(((bf16[8,1,128,128]{3,2,1,0:T(8,128)(2,1)}), bf16[64,1,128,128]{3,2,1,0:T(8,128)(2,1)}) %all-gather.55.cloned.1.call-update) | async-done | bytes 2097168 | tf_op jit(solution)/shard_map/all_gather | solution.py:11
  468.6 71.1 %all-gather.57.cloned.1.call-done = bf16[32768,128]{0,1:T(8,128)(2,1)} async-done(((bf16[2048,128]{0,1:T(8,128)(2,1)}), bf16[32768,128]{0,1:T(8,128)(2,1)}) %all-gather.57.cloned.1.call-update) | async-done | bytes 8388624 | tf_op jit(solution)/shard_map/all_gather | solution.py:11
  539.7 12.9 copy.114
  601.3 21.1 %all-gather.59.cloned.1.call-done = bf16[64,1,128,128]{3,2,1,0:T(8,128)(2,1)} async-done(((bf16[8,1,128,128]{3,2,1,0:T(8,128)(2,1)}), bf16[64,1,128,128]{3,2,1,0:T(8,128)(2,1)}) %all-gather.59.cloned.1.call-update) | async-done | bytes 2097168 | tf_op jit(solution)/shard_map/all_gather | solution.py:11
  636.2 70.9 %all-gather.61.cloned.1.call-done = bf16[32768,128]{0,1:T(8,128)(2,1)} async-done(((bf16[2048,128]{0,1:T(8,128)(2,1)}), bf16[32768,128]{0,1:T(8,128)(2,1)}) %all-gather.61.cloned.1.call-update) | async-done | bytes 8388624 | tf_op jit(solution)/shard_map/all_gather | solution.py:11
  707.1 12.9 copy.116
  768.7 21.0 %all-gather.63.cloned.1.call-done = bf16[64,1,128,128]{3,2,1,0:T(8,128)(2,1)} async-done(((bf16[8,1,128,128]{3,2,1,0:T(8,128)(2,1)}), bf16[64,1,128,128]{3,2,1,0:T(8,128)(2,1)}) %all-gather.63.cloned.1.call-update) | async-done | bytes 2097168 | tf_op jit(solution)/shard_map/all_gather | solution.py:11
  803.4 71.1 %all-gather.65.cloned.1.call-done = bf16[32768,128]{0,1:T(8,128)(2,1)} async-done(((bf16[2048,128]{0,1:T(8,128)(2,1)}), bf16[32768,128]{0,1:T(8,128)(2,1)}) %all-gather.65.cloned.1.call-update) | async-done | bytes 8388624 | tf_op jit(solution)/shard_map/all_gather | solution.py:11
  874.5 12.9 copy.118
  895.0 12.6 all-gather.15
  936.3 21.0 %all-gather.67.cloned.1.call-done = bf16[64,1,128,128]{3,2,1,0:T(8,128)(2,1)} async-done(((bf16[8,1,128,128]{3,2,1,0:T(8,128)(2,1)}), bf16[64,1,128,128]{3,2,1,0:T(8,128)(2,1)}) %all-gather.67.cloned.1.call-update) | async-done | bytes 2097168 | tf_op jit(solution)/shard_map/all_gather | solution.py:11
  970.9 71.1 %all-gather.69.cloned.1.call-done = bf16[32768,128]{0,1:T(8,128)(2,1)} async-done(((bf16[2048,128]{0,1:T(8,128)(2,1)}), bf16[32768,128]{0,1:T(8,128)(2,1)}) %all-gather.69.cloned.1.call-update) | async-done | bytes 8388624 | tf_op jit(solution)/shard_map/all_gather | solution.py:11
  1042.1 12.9 copy.120
  1103.7 21.0 %all-gather.71.cloned.1.call-done = bf16[64,1,128,128]{3,2,1,0:T(8,128)(2,1)} async-done(((bf16[8,1,128,128]{3,2,1,0:T(8,128)(2,1)}), bf16[64,1,128,128]{3,2,1,0:T(8,128)(2,1)}) %all-gather.71.cloned.1.call-update) | async-done | bytes 2097168 | tf_op jit(solution)/shard_map/all_gather | solution.py:11
  1138.6 70.9 %all-gather.73.cloned.1.call-done = bf16[32768,128]{0,1:T(8,128)(2,1)} async-done(((bf16[2048,128]{0,1:T(8,128)(2,1)}), bf16[32768,128]{0,1:T(8,128)(2,1)}) %all-gather.73.cloned.1.call-update) | async-done | bytes 8388624 | tf_op jit(solution)/shard_map/all_gather | solution.py:11
  1209.5 12.9 copy.122
  1271.0 21.1 %all-gather.75.cloned.1.call-done = bf16[64,1,128,128]{3,2,1,0:T(8,128)(2,1)} async-done(((bf16[8,1,128,128]{3,2,1,0:T(8,128)(2,1)}), bf16[64,1,128,128]{3,2,1,0:T(8,128)(2,1)}) %all-gather.75.cloned.1.call-update) | async-done | bytes 2097168 | tf_op jit(solution)/shard_map/all_gather | solution.py:11
  1305.7 71.1 %all-gather.77.cloned.1.call-done = bf16[32768,128]{0,1:T(8,128)(2,1)} async-done(((bf16[2048,128]{0,1:T(8,128)(2,1)}), bf16[32768,128]{0,1:T(8,128)(2,1)}) %all-gather.77.cloned.1.call-update) | async-done | bytes 8388624 | tf_op jit(solution)/shard_map/all_gather | solution.py:11
  1376.8 12.9 copy.124
  1397.3 12.5 all-gather.24
  1438.5 21.0 %all-gather.79.cloned.1.call-done = bf16[64,1,128,128]{3,2,1,0:T(8,128)(2,1)} async-done(((bf16[8,1,128,128]{3,2,1,0:T(8,128)(2,1)}), bf16[64,1,128,128]{3,2,1,0:T(8,128)(2,1)}) %all-gather.79.cloned.1.call-update) | async-done | bytes 2097168 | tf_op jit(solution)/shard_map/all_gather | solution.py:11
  1474.3 13.3 copy.86
  (249 shorter events, 506.8 us)
Async XLA Ops:
  6.5 50.5 %all-gather.45.cloned.1.call-start = ((), (), s32[]{:S(2)}) async-start(), calls=%async_computation | async-start | bytes 2228224 | tf_op jit(solution)/shard_map/all_gather | solution.py:31
  7.3 84.5 %all-gather.47.cloned.1.call-start = ((), (), s32[]{:S(2)}) async-start(), calls=%async_computation.1 | async-start | bytes 4718592 | tf_op jit(solution)/shard_map/all_gather | solution.py:47
  60.3 144.4 %all-gather.49.cloned.1.call-start = ((), (), s32[]{:S(2)}) async-start(), calls=%async_computation.2 | async-start | bytes 8912896 | tf_op jit(solution)/shard_map/all_gather | solution.py:11
  69.2 9.3 copy-start.7
  133.7 153.7 %all-gather.51.cloned.1.call-start = ((), (), s32[]{:S(2)}) async-start(), calls=%async_computation.3 | async-start | bytes 2359296 | tf_op jit(solution)/shard_map/all_gather | solution.py:11
  263.3 108.9 %all-gather.53.cloned.1.call-start = ((), (), s32[]{:S(2)}) async-start(), calls=%async_computation.4 | async-start | bytes 8912896 | tf_op jit(solution)/shard_map/all_gather | solution.py:11
  295.7 3.4 copy-start.1
  300.7 154.3 %all-gather.55.cloned.1.call-start = ((), (), s32[]{:S(2)}) async-start(), calls=%async_computation.5 | async-start | bytes 2359296 | tf_op jit(solution)/shard_map/all_gather | solution.py:11
  430.9 108.8 %all-gather.57.cloned.1.call-start = ((), (), s32[]{:S(2)}) async-start(), calls=%async_computation.6 | async-start | bytes 8912896 | tf_op jit(solution)/shard_map/all_gather | solution.py:11
  463.3 3.4 copy-start.2
  468.3 154.1 %all-gather.59.cloned.1.call-start = ((), (), s32[]{:S(2)}) async-start(), calls=%async_computation.7 | async-start | bytes 2359296 | tf_op jit(solution)/shard_map/all_gather | solution.py:11
  598.3 108.9 %all-gather.61.cloned.1.call-start = ((), (), s32[]{:S(2)}) async-start(), calls=%async_computation.8 | async-start | bytes 8912896 | tf_op jit(solution)/shard_map/all_gather | solution.py:11
  630.7 3.4 copy-start.3
  635.7 154.1 %all-gather.63.cloned.1.call-start = ((), (), s32[]{:S(2)}) async-start(), calls=%async_computation.9 | async-start | bytes 2359296 | tf_op jit(solution)/shard_map/all_gather | solution.py:11
  765.6 108.8 %all-gather.65.cloned.1.call-start = ((), (), s32[]{:S(2)}) async-start(), calls=%async_computation.10 | async-start | bytes 8912896 | tf_op jit(solution)/shard_map/all_gather | solution.py:11
  798.0 3.4 copy-start.4
  803.0 154.3 %all-gather.67.cloned.1.call-start = ((), (), s32[]{:S(2)}) async-start(), calls=%async_computation.11 | async-start | bytes 2359296 | tf_op jit(solution)/shard_map/all_gather | solution.py:11
  933.2 108.9 %all-gather.69.cloned.1.call-start = ((), (), s32[]{:S(2)}) async-start(), calls=%async_computation.12 | async-start | bytes 8912896 | tf_op jit(solution)/shard_map/all_gather | solution.py:11
  965.6 3.4 copy-start.5
  970.6 154.1 %all-gather.71.cloned.1.call-start = ((), (), s32[]{:S(2)}) async-start(), calls=%async_computation.13 | async-start | bytes 2359296 | tf_op jit(solution)/shard_map/all_gather | solution.py:11
  1100.6 108.8 %all-gather.73.cloned.1.call-start = ((), (), s32[]{:S(2)}) async-start(), calls=%async_computation.14 | async-start | bytes 8912896 | tf_op jit(solution)/shard_map/all_gather | solution.py:11
  1133.0 3.4 copy-start.6
  1138.0 154.1 %all-gather.75.cloned.1.call-start = ((), (), s32[]{:S(2)}) async-start(), calls=%async_computation.15 | async-start | bytes 2359296 | tf_op jit(solution)/shard_map/all_gather | solution.py:11
  1268.0 108.9 %all-gather.77.cloned.1.call-start = ((), (), s32[]{:S(2)}) async-start(), calls=%async_computation.16 | async-start | bytes 8912896 | tf_op jit(solution)/shard_map/all_gather | solution.py:11
  1300.3 3.4 copy-start
  1305.4 154.1 %all-gather.79.cloned.1.call-start = ((), (), s32[]{:S(2)}) async-start(), calls=%async_computation.17 | async-start | bytes 2359296 | tf_op jit(solution)/shard_map/all_gather | solution.py:11
Sparse Core Ops, SparseCore 0:
  9.5 47.4 all-gather.44
  60.4 31.3 all-gather.46
  133.9 70.8 all-gather.48
  263.4 23.9 all-gather.50
  300.8 71.2 all-gather.52
  431.0 23.9 all-gather.54
  468.4 71.2 all-gather.56
  598.4 23.9 all-gather.58
  635.8 71.2 all-gather.60
  765.8 23.9 all-gather.62
  803.1 71.2 all-gather.64
  933.3 23.9 all-gather.66
  970.7 71.2 all-gather.68
  1100.7 23.9 all-gather.70
  1138.1 71.2 all-gather.72
  1268.1 23.9 all-gather.74
  1305.5 71.2 all-gather.76
  1435.5 23.9 all-gather.78
